TPU v7x, 512 devices: a whole 4x4x16 slice. The times are simulated.
512 devices in a mesh: rep: 16 (over x, z_lo), mp: 32 (over z_hi, y, core).
Axes of the slice: x: 4, y: 4, z: 16 (z_hi: 4, z_lo: 4; z = z_hi * 4 + z_lo), core: 2. Of those that a mesh axis runs over, the one named last changes fastest.
Arguments:
- dense_feats: bfloat16 [65536, 13], P(('rep', 'mp')), may hold values from -6 to 6
- bag_counts: int32 [65536, 32, 64], P('rep', 'mp'), may hold values from 0 to 2
- emb_rows: bfloat16 [32, 64, 256], P('mp'), may hold values from -0.625 to 0.625
- v_emb: bfloat16 [8192, 256], P('mp'), may hold values from -0.0625 to 0.0625
- u_emb: bfloat16 [256, 8192], P(None, 'mp'), may hold values from -0.375 to 0.375
- b_emb: bfloat16 [8192], P('mp'), may hold values from -3 to 3
- v_bot: bfloat16 [256, 256], replicated, may hold values from -0.375 to 0.375
- u_bot: bfloat16 [256, 256], replicated, may hold values from -0.375 to 0.375
- b_bot: bfloat16 [256], replicated, may hold values from -3 to 3
- w_first: bfloat16 [13, 1024], replicated, may hold values from -1.75 to 1.75
- b_first: bfloat16 [1024], replicated, may hold values from -3 to 3
- w_second: bfloat16 [1024, 256], replicated, may hold values from -0.1875 to 0.1875
- b_second: bfloat16 [256], replicated, may hold values from -3 to 3
- cot_cross: bfloat16 [65536, 8192], P(('rep', 'mp')), may hold values from -24 to 24
- cot_bottom: bfloat16 [65536, 256], P(('rep', 'mp')), may hold values from -6 to 6
Outputs:
- cross_emb: bfloat16 [65536, 8192], P(('rep', 'mp'))
- cross_bot: bfloat16 [65536, 256], P(('rep', 'mp'))
- grad_table: bfloat16 [32, 64, 256], P('mp')
- grad_v_emb: bfloat16 [8192, 256], P('mp')
- grad_u_emb: bfloat16 [256, 8192], P(None, 'mp')
- grad_b_emb: bfloat16 [8192], P('mp')
- grad_v_bot: bfloat16 [256, 256], replicated
- grad_u_bot: bfloat16 [256, 256], replicated
- grad_b_bot: bfloat16 [256], replicated
- grad_w_first: bfloat16 [13, 1024], replicated
- grad_b_first: bfloat16 [1024], replicated
- grad_w_second: bfloat16 [1024, 256], replicated
- grad_b_second: bfloat16 [256], replicated
Inputs may be any that keep to these rules, and one draw needn't show every extreme that they name: bag_counts[s, t, j] is how often row j of table t occurs in the bag of sample s.
All inputs are finite; a program needn't handle non-finite values.
Results may differ from a plain program's by a relative error of at most 0.029.
Values may be sent and summed in bfloat16 or wider, within the bound.
A program may use at most 64 MiB of HBM per device.

v0:
```python
import math
import jax
import jax.numpy as jnp
from jax import lax
from jax.sharding import PartitionSpec as P


def silu_slope(inputs):
    gate_value = jax.nn.sigmoid(inputs)
    return gate_value * (1.0 + inputs * (1.0 - gate_value))


def contract_rows(left_side, right_side):
    return lax.dot_general(
        left_side, right_side, (((0,), (0,)), ((), ())), preferred_element_type=jnp.float32
    )


def contract_cols(left_side, right_side):
    return lax.dot_general(
        left_side, right_side, (((1,), (1,)), ((), ())), preferred_element_type=jnp.float32
    )


def local(
    dense_feats,
    bag_counts,
    emb_rows,
    v_emb,
    u_emb,
    b_emb,
    v_bot,
    u_bot,
    b_bot,
    w_first,
    b_first,
    w_second,
    b_second,
    cot_cross,
    cot_bottom,
):
    tables = lax.axis_size("mp")
    replicas = lax.axis_size("rep")
    own_rows = dense_feats.shape[0]
    table_rows, width = emb_rows.shape[1:]
    rank = v_emb.shape[1]
    share = width // replicas
    grad_scale = 1.0 / math.sqrt(own_rows * tables * replicas)
    first = lax.axis_index("rep") * share
    pad = -(table_rows + 1) % 128
    packed = jnp.concatenate(
        [v_emb, u_emb.T, emb_rows[0].T, b_emb[:, None], jnp.zeros((width, pad), jnp.bfloat16)],
        axis=1,
    )
    packed = lax.dynamic_slice_in_dim(packed, first, share, 0)
    packed = lax.all_gather(packed, ("mp", "rep"), axis=0, tiled=True)
    counts = bag_counts[:, 0, :].astype(jnp.bfloat16)
    counts = jnp.swapaxes(counts.reshape(tables, own_rows, table_rows), 1, 2)
    counts = lax.all_to_all(counts, "mp", split_axis=0, concat_axis=0, tiled=True)
    first_pre = jnp.dot(dense_feats, w_first, preferred_element_type=jnp.float32) + b_first.astype(
        jnp.float32
    )
    first_act = jax.nn.silu(first_pre).astype(jnp.bfloat16)
    second_pre = jnp.dot(first_act, w_second, preferred_element_type=jnp.float32) + b_second.astype(
        jnp.float32
    )
    bottom = jax.nn.silu(second_pre).astype(jnp.bfloat16)
    v_all = packed[:, :rank]
    u_all = packed[:, rank : 2 * rank]
    emb_all = packed[:, 2 * rank : 2 * rank + table_rows].reshape(tables, width, table_rows)
    b_all = packed[:, 2 * rank + table_rows].reshape(1, tables * width).astype(jnp.float32)
    pooled = lax.dot_general(
        counts, emb_all, (((1,), (2,)), ((0,), (0,))), preferred_element_type=jnp.float32
    ).astype(jnp.bfloat16)
    pooled = jnp.swapaxes(pooled, 0, 1).reshape(own_rows, tables * width)
    low_rank = (
        jnp.dot(pooled, v_all, preferred_element_type=jnp.float32)
        + jnp.dot(bottom, v_bot, preferred_element_type=jnp.float32)
    ).astype(jnp.bfloat16)
    lift_emb = contract_cols(low_rank, u_all) + b_all
    pooled_full = pooled.astype(jnp.float32)
    cross_emb = (pooled_full * (lift_emb + 1.0)).astype(jnp.bfloat16)
    lift_bottom = jnp.dot(low_rank, u_bot, preferred_element_type=jnp.float32) + b_bot.astype(
        jnp.float32
    )
    bottom_full = bottom.astype(jnp.float32)
    cross_bot = (bottom_full * (lift_bottom + 1.0)).astype(jnp.bfloat16)
    cot_rows = cot_cross.astype(jnp.float32)
    d_lift = cot_rows * pooled_full
    d_lift_round = d_lift.astype(jnp.bfloat16)
    cot_low = cot_bottom.astype(jnp.float32)
    d_bottom_lift = cot_low * bottom_full
    d_bottom_round = d_bottom_lift.astype(jnp.bfloat16)
    d_low = (
        jnp.dot(d_lift_round, u_all, preferred_element_type=jnp.float32)
        + contract_cols(d_bottom_round, u_bot)
    ).astype(jnp.bfloat16)
    d_pooled = (cot_rows * (lift_emb + 1.0) + contract_cols(d_low, v_all)).astype(jnp.bfloat16)
    d_tables = jnp.swapaxes(d_pooled.reshape(own_rows, tables, width), 0, 1)
    grad_table = lax.dot_general(
        d_tables, counts, (((1,), (2,)), ((0,), (0,))), preferred_element_type=jnp.float32
    ).reshape(tables * width, table_rows)
    grad_v = contract_rows(pooled, d_low)
    grad_u = contract_rows(d_lift_round, low_rank)
    grad_b = jnp.sum(d_lift, axis=0)
    grads = jnp.concatenate(
        [
            grad_v.astype(jnp.bfloat16),
            grad_u.astype(jnp.bfloat16),
            grad_table.astype(jnp.bfloat16),
            grad_b.astype(jnp.bfloat16)[:, None],
            jnp.zeros((tables * width, pad), jnp.bfloat16),
        ],
        axis=1,
    )
    columns = grads.shape[1]
    grads = jnp.swapaxes(grads.reshape(tables, replicas, share, columns), 0, 1)
    grads = lax.psum_scatter(
        grads.reshape(replicas * tables * share, columns), "rep", scatter_dimension=0, tiled=True
    )
    grads = lax.psum_scatter(
        grads.astype(jnp.float32) * grad_scale, "mp", scatter_dimension=0, tiled=True
    )
    grads = lax.optimization_barrier(grads).astype(jnp.bfloat16)
    grads = lax.all_gather(grads, "rep", axis=0, tiled=True)
    d_bottom = cot_low * (lift_bottom + 1.0) + contract_cols(d_low, v_bot)
    grad_vb = grad_scale * contract_rows(bottom, d_low)
    grad_ub = grad_scale * contract_rows(low_rank, d_bottom_round)
    grad_bb = grad_scale * jnp.sum(d_bottom_lift, axis=0)
    d_second = d_bottom * silu_slope(second_pre)
    d_second_round = d_second.astype(jnp.bfloat16)
    grad_ws = grad_scale * contract_rows(first_act, d_second_round)
    grad_bs = grad_scale * jnp.sum(d_second, axis=0)
    d_first = contract_cols(d_second_round, w_second) * silu_slope(first_pre)
    d_first_round = d_first.astype(jnp.bfloat16)
    grad_wf = grad_scale * contract_rows(dense_feats, d_first_round)
    grad_bf = grad_scale * jnp.sum(d_first, axis=0)
    dense_sums = lax.psum(
        (grad_wf, grad_bf, grad_ws, grad_bs, grad_vb, grad_ub, grad_bb), ("rep", "mp")
    )
    return (
        cross_emb,
        cross_bot,
        grads[:, 2 * rank : 2 * rank + table_rows].T[None],
        grads[:, :rank],
        grads[:, rank : 2 * rank].T,
        grads[:, 2 * rank + table_rows],
        dense_sums[4].astype(jnp.bfloat16),
        dense_sums[5].astype(jnp.bfloat16),
        dense_sums[6].astype(jnp.bfloat16),
        dense_sums[0].astype(jnp.bfloat16),
        dense_sums[1].astype(jnp.bfloat16),
        dense_sums[2].astype(jnp.bfloat16),
        dense_sums[3].astype(jnp.bfloat16),
    )


def solution(mesh):
    return jax.shard_map(
        local,
        mesh=mesh,
        in_specs=(
            P(("rep", "mp"), None),
            P("rep", "mp", None),
            P("mp", None, None),
            P("mp", None),
            P(None, "mp"),
            P("mp"),
            P(),
            P(),
            P(),
            P(),
            P(),
            P(),
            P(),
            P(("rep", "mp"), None),
            P(("rep", "mp"), None),
        ),
        out_specs=(
            P(("rep", "mp"), None),
            P(("rep", "mp"), None),
            P("mp", None, None),
            P("mp", None),
            P(None, "mp"),
            P("mp"),
            P(),
            P(),
            P(),
            P(),
            P(),
            P(),
            P(),
        ),
        check_vma=False,
    )
```

profile of v0, /device:TPU:8, one launch (start us, length us, event | category | flops | bytes accessed | tf_op | source)
XLA Modules:
  0.0 1927.5 jit_solution(6832458507843473368)
XLA Ops:
  7.3 1.1 copy.72
  8.4 0.9 copy.73
  9.3 0.8 broadcast_in_dim.20
  10.1 1.0 concatenate.11
  11.1 0.6 constant_dynamic-slice_fusion
  11.8 1.3 convert_bitcast_fusion
  13.2 1.0 copy.98
  14.2 18.3 all-to-all-start
  32.6 0.3 convolution_add_fusion.2
  32.9 0.8 copy-done.5
  33.7 1.5 fusion.23
  35.2 1388.3 %all-gather.2.cloned.1.call-done = bf16[8192,640]{1,0:T(8,128)(2,1)} async-done(((bf16[16,640]{1,0:T(8,128)(2,1)}), bf16[8192,640]{1,0:T(8,128)(2,1)}) %all-gather.2.cloned.1.call-update) | async-done | bytes 10485776 | tf_op jit(solution)/shard_map/all_gather | solution.py:56
  1423.6 1.6 slice-done.3
  1425.2 2.0 convolution_convert_fusion.2
  1427.2 2.9 copy.78
  1430.1 3.8 fusion.9
  1434.1 3.4 convolution_convert_fusion
  1437.6 4.0 fusion.5
  1441.6 0.2 fusion.17
  1441.8 3.3 convolution_convert_fusion.1
  1445.1 1.4 convert_reduce_fusion
  1446.5 3.0 fusion.3
  1449.5 1.6 fusion.1
  1451.1 0.5 fusion.13
  1451.5 1.8 copy.80
  1453.3 2.1 copy.83
  1455.6 4.2 copy.84
  1459.8 4.8 copy.82
  1464.6 2.5 copy.81
  1467.2 1.7 broadcast_in_dim.18
  1468.9 18.8 concatenate.14
  1487.7 0.3 reduce-scatter.5.cloned.1.call-start
  1488.0 0.3 copy-done.16
  1488.3 0.8 fusion.22
  1489.1 265.8 %reduce-scatter.3.cloned.1.call-done = bf16[512,640]{1,0:T(8,128)(2,1)} async-done(((bf16[8192,640]{1,0:T(8,128)(2,1)}), bf16[512,640]{1,0:T(8,128)(2,1)}) %reduce-scatter.3.cloned.1.call-update) | async-done | bytes 655376 | tf_op jit(solution)/shard_map/reduce_scatter | solution.py:118
  1754.9 2.3 convert_multiply_fusion.3
  1757.2 0.2 fusion.30
  1757.5 0.4 fusion.29
  1758.0 0.4 convolution_multiply_fusion
  1758.4 0.2 convolution_multiply_fusion.3
  1758.6 0.2 convolution_multiply_fusion.2
  1758.8 114.1 %all-reduce.2 = (bf16[256,256]{1,0:T(8,128)(2,1)}, bf16[256,256]{1,0:T(8,128)(2,1)}, bf16[256]{0:T(256)(128)(2,1)}, bf16[13,1024]{1,0:T(8,128)(2,1)}, bf16[1024]...) all-reduce(f32[256,256]{1,0:T(8,128)S(1)} %convolution_multiply_fus, ...), channel_id=1, replica_groups=mesh['rep'=16,'mp'=32] {'rep','mp'}, use_global_device_ids=true, to_apply=%region_3.4 | all-reduce | flops 408064 | bytes 2448384 | tf_op jit(solution)/shard_map/psum | solution.py:138
  1873.0 0.8 convert_element_type.162
  1873.7 44.4 %all_gather.7 = bf16[256,640]{1,0:T(8,128)(2,1)S(1)} all-gather(bf16[16,640]{1,0:T(8,128)(2,1)S(1)} %convert_element_type.162), channel_id=1, replica_groups=mesh['rep'=16,'mp'=32] {'rep'}, dimensions={0}, use_global_device_ids=true | all-gather | bytes 348160 | tf_op jit(solution)/shard_map/all_gather | solution.py:125
  1918.1 0.7 slice_bitcast_fusion
  1918.8 0.7 slice_reduce_fusion
  1919.5 0.8 copy.86
  1920.2 0.7 copy.85
  (60 shorter events, 0.9 us)
Async XLA Ops:
  7.2 26.5 %copy-start = (bf16[1024,256]{1,0:T(8,128)(2,1)S(1)}, bf16[1024,256]{1,0:T(8,128)(2,1)}, u32[]{:S(2)}) copy-start(bf16[1024,256]{1,0:T(8,128)(2,1)} %param.26) | copy-start | bytes 1572868
  7.2 25.4 %copy-start.13 = (bf16[1024]{0:T(1024)(128)(2,1)S(1)}, bf16[1024]{0:T(1024)(128)(2,1)}, u32[]{:S(2)}) copy-start(bf16[1024]{0:T(1024)(128)(2,1)} %param.25) | copy-start | bytes 6148
  7.2 25.4 %copy-start.15 = (bf16[256]{0:T(256)(128)(2,1)S(1)}, bf16[256]{0:T(256)(128)(2,1)}, u32[]{:S(2)}) copy-start(bf16[256]{0:T(256)(128)(2,1)} %param.27) | copy-start | bytes 1540
  7.2 25.4 %copy-start.11 = (bf16[128,13]{0,1:T(8,128)(2,1)S(1)}, bf16[128,13]{0,1:T(8,128)(2,1)}, u32[]{:S(2)}) copy-start(bf16[128,13]{0,1:T(8,128)(2,1)} %param.15) | copy-start | bytes 9988
  7.2 25.4 %copy-start.10 = (bf16[13,1024]{1,0:T(8,128)(2,1)S(1)}, bf16[13,1024]{1,0:T(8,128)(2,1)}, u32[]{:S(2)}) copy-start(bf16[13,1024]{1,0:T(8,128)(2,1)} %param.24) | copy-start | bytes 79876
  7.2 26.5 %copy-start.7 = (bf16[128,256]{1,0:T(8,128)(2,1)S(1)}, bf16[128,256]{1,0:T(8,128)(2,1)}, u32[]{:S(2)}) copy-start(bf16[128,256]{1,0:T(8,128)(2,1)} %param.29) | copy-start | bytes 196612
  7.2 1416.3 %all-gather.2.cloned.1.call-start = ((), (), s32[]{:S(2)}) async-start(), calls=%async_computation.3 | async-start | bytes 10506240 | tf_op jit(solution)/shard_map/all_gather | solution.py:56
  14.2 1409.4 %all-to-all-start = ((bf16[32,64,128]{2,1,0:T(8,128)(2,1)}), bf16[32,64,128]{2,1,0:T(8,128)(2,1)S(1)}, u32[]{:S(2)}, u32[]{:S(2)}) async-start(bf16[32,64,128]{2,1,0:T(8,128)(2,1)} %bitcast.68), calls=%async_computation | async-start | bytes 1048576 | tf_op jit(solution)/shard_map/all_to_all | solution.py:59
  32.5 1722.4 %reduce-scatter.3.cloned.1.call-start = ((), (), s32[]{:S(2)}) async-start(), calls=%async_computation.4 | async-start | bytes 11141120 | tf_op jit(solution)/shard_map/reduce_scatter | solution.py:118
  32.9 0.8 copy-start.5
  1423.6 1.6 slice-start.3
  1430.1 3.9 copy-start.8
  1430.1 4.0 copy-start.1
  1434.1 11.0 slice-start
  1434.1 11.0 slice-start.1
  1437.6 4.0 copy-start.4
  1437.6 4.2 copy-start.3
  1437.6 7.5 slice-start.2
  1459.8 4.8 copy-start.2
  1487.7 0.7 copy-start.16
  1487.7 269.5 %copy-start.9 = (bf16[256,256]{1,0:T(8,128)(2,1)S(1)}, bf16[256,256]{1,0:T(8,128)(2,1)}, u32[]{:S(2)}) copy-start(bf16[256,256]{1,0:T(8,128)(2,1)} %param.21) | copy-start | bytes 393220
  1487.7 269.5 %copy-start.17 = (f32[128,256]{1,0:T(8,128)S(1)}, f32[128,256]{1,0:T(8,128)}, u32[]{:S(2)}) copy-start(f32[128,256]{1,0:T(8,128)} %get-tuple-element.91) | copy-start | bytes 393220
  1487.7 269.8 %copy-start.14 = (f32[256]{0:T(256)S(1)}, f32[256]{0:T(256)}, u32[]{:S(2)}) copy-start(f32[256]{0:T(256)} %get-tuple-element.85) | copy-start | bytes 3076
  1487.7 269.8 %copy-start.6 = (f32[128,1024]{1,0:T(8,128)S(1)}, f32[128,1024]{1,0:T(8,128)}, u32[]{:S(2)}) copy-start(f32[128,1024]{1,0:T(8,128)} %copy-done.5) | copy-start | bytes 1572868
  1487.7 270.1 %copy-start.12 = (bf16[128,13]{0,1:T(8,128)(2,1)S(1)}, bf16[128,13]{0,1:T(8,128)(2,1)}, u32[]{:S(2)}) copy-start(bf16[128,13]{0,1:T(8,128)(2,1)} %param.15) | copy-start | bytes 9988
  1487.7 385.2 %reduce-scatter.5.cloned.1.call-start = ((), (), s32[]{:S(2)}) async-start(), calls=%async_computation.5 | async-start | bytes 1351680 | tf_op jit(solution)/shard_map/reduce_scatter | solution.py:121
Sparse Core Ops, SparseCore 0:
  11.9 1411.6 all-gather.1
  1487.8 267.0 reduce-scatter.2
  1759.3 113.5 reduce-scatter.4
where the time goes:
time: 1930 us
  waiting for transfers between devices  1650 us (85%)
  blocking collectives  158 us (8%)
  local copies, waits for them, and re-layouts  50.2 us (3%)
  matrix products  26 us (1%)
    all_gather x1, waiting for transfers between devices, local(): packed = lax.all_gather(packed, ('mp', 'rep'), axis=0, tiled=True)  1390 us
    reduce_scatter x1, waiting for transfers between devices, local(): lax.psum_scatter(grads.reshape(replicas * tables * share, columns), 'rep'...  266 us
    psum x1, blocking collectives, local(): lax.psum((grad_wf, grad_bf, grad_ws, grad_bs, grad_vb, grad_ub, grad_bb),...  114 us
    all_gather x1, blocking collectives, local(): grads = lax.all_gather(grads, 'rep', axis=0, tiled=True)  44.4 us
  transfers between devices with their start and end apart: 4, of which 3 were waited for; matrix products, arithmetic and copies ran while one was open for 0% of the time, Pallas kernels for 0%

commit v1 on v0

--- a/solution.py
+++ b/solution.py
@@ -122,7 +122,9 @@
         grads.astype(jnp.float32) * grad_scale, "mp", scatter_dimension=0, tiled=True
     )
     grads = lax.optimization_barrier(grads).astype(jnp.bfloat16)
-    grads = lax.all_gather(grads, "rep", axis=0, tiled=True)
+    grads = jnp.concatenate(
+        lax.all_to_all(jnp.stack([grads] * lax.axis_size("rep")), "rep", 0, 0), axis=0
+    )
     d_bottom = cot_low * (lift_bottom + 1.0) + contract_cols(d_low, v_bot)
     grad_vb = grad_scale * contract_rows(bottom, d_low)
     grad_ub = grad_scale * contract_rows(low_rank, d_bottom_round)

time: 1930 us -> 2000 us (1.036)
  the two profiles are of different devices: /device:TPU:8 before, /device:TPU:1 now
where the time goes in v1:
time: 2000 us
  waiting for transfers between devices  1770 us (88%)
  blocking collectives  114 us (6%)
  local copies, waits for them, and re-layouts  50.7 us (3%)
  matrix products  26 us (1%)
  starting transfers between devices  23.9 us (1%)
    all_gather x1, waiting for transfers between devices, local(): packed = lax.all_gather(packed, ('mp', 'rep'), axis=0, tiled=True)  1410 us
    reduce_scatter x1, waiting for transfers between devices, local(): lax.psum_scatter(grads.reshape(replicas * tables * share, columns), 'rep'...  241 us
    psum x1, blocking collectives, local(): lax.psum((grad_wf, grad_bf, grad_ws, grad_bs, grad_vb, grad_ub, grad_bb),...  114 us
    reduce_scatter x1, waiting for transfers between devices, local(): lax.psum_scatter(grads.astype(jnp.float32) * grad_scale, 'mp', scatter_di...  113 us
  transfers between devices with their start and end apart: 5, of which 3 were waited for; matrix products, arithmetic and copies ran while one was open for 0% of the time, Pallas kernels for 0%

profile of v1, /device:TPU:1, one launch (start us, length us, event | category | flops | bytes accessed | tf_op | source)
XLA Modules:
  0.0 2003.0 jit_solution(8442828560587823694)
XLA Ops:
  7.3 1.1 copy.71
  8.4 0.9 copy.72
  9.3 0.8 broadcast_in_dim.20
  10.1 1.0 concatenate.11
  11.1 0.6 constant_dynamic-slice_fusion
  11.8 1.3 convert_bitcast_fusion
  13.2 1.0 copy.97
  14.2 19.4 all-to-all-start
  33.7 0.2 convolution_add_fusion.2
  33.9 0.8 copy-done.5
  34.8 1.5 fusion.23
  36.3 1414.0 %all-gather.2.cloned.1.call-done = bf16[8192,640]{1,0:T(8,128)(2,1)} async-done(((bf16[16,640]{1,0:T(8,128)(2,1)}), bf16[8192,640]{1,0:T(8,128)(2,1)}) %all-gather.2.cloned.1.call-update) | async-done | bytes 10485776 | tf_op jit(solution)/shard_map/all_gather | solution.py:56
  1450.3 1.6 slice-done.3
  1451.9 2.0 convolution_convert_fusion.2
  1453.9 2.9 copy.77
  1456.8 3.8 fusion.9
  1460.9 3.4 convolution_convert_fusion
  1464.3 4.0 fusion.5
  1468.3 0.2 fusion.17
  1468.5 3.3 convolution_convert_fusion.1
  1471.8 1.4 convert_reduce_fusion
  1473.2 3.0 fusion.3
  1476.3 1.6 fusion.1
  1477.8 0.5 fusion.13
  1478.3 1.8 copy.79
  1480.0 2.1 copy.82
  1482.3 4.2 copy.83
  1486.5 4.8 copy.81
  1491.4 2.5 copy.80
  1493.9 1.7 broadcast_in_dim.18
  1495.6 18.8 concatenate.14
  1514.6 241.1 %reduce-scatter.3.cloned.1.call-done = bf16[512,640]{1,0:T(8,128)(2,1)} async-done(((bf16[8192,640]{1,0:T(8,128)(2,1)}), bf16[512,640]{1,0:T(8,128)(2,1)}) %reduce-scatter.3.cloned.1.call-update) | async-done | bytes 655376 | tf_op jit(solution)/shard_map/reduce_scatter | solution.py:118
  1755.7 2.3 convert_multiply_fusion.3
  1758.0 0.8 fusion.22
  1758.8 0.2 fusion.30
  1759.0 0.4 fusion.29
  1759.4 113.2 %reduce-scatter.5.cloned.1.call-done = f32[16,640]{1,0:T(8,128)} async-done(((f32[512,640]{1,0:T(8,128)}), f32[16,640]{1,0:T(8,128)}) %reduce-scatter.5.cloned.1.call-update) | async-done | bytes 40976 | tf_op jit(solution)/shard_map/reduce_scatter | solution.py:121
  1872.6 0.8 convert_element_type.162
  1873.4 0.8 stack.2
  1874.2 4.4 all-to-all-start.1
  1878.7 0.4 convolution_multiply_fusion
  1879.1 0.2 convolution_multiply_fusion.3
  1879.3 0.2 convolution_multiply_fusion.2
  1879.5 114.0 %all-reduce.2 = (bf16[256,256]{1,0:T(8,128)(2,1)}, bf16[256,256]{1,0:T(8,128)(2,1)}, bf16[256]{0:T(256)(128)(2,1)}, bf16[13,1024]{1,0:T(8,128)(2,1)}, bf16[1024]...) all-reduce(f32[256,256]{1,0:T(8,128)S(1)} %convolution_multiply_fus, ...), channel_id=1, replica_groups=mesh['rep'=16,'mp'=32] {'rep','mp'}, use_global_device_ids=true, to_apply=%region_3.4 | all-reduce | flops 408064 | bytes 2448384 | tf_op jit(solution)/shard_map/psum | solution.py:140
  1993.6 0.7 slice_bitcast_fusion
  1994.3 0.7 slice_reduce_fusion
  1995.0 0.8 copy.85
  1995.7 0.7 copy.84
  (62 shorter events, 0.8 us)
Async XLA Ops:
  7.2 27.6 %copy-start = (bf16[1024,256]{1,0:T(8,128)(2,1)S(1)}, bf16[1024,256]{1,0:T(8,128)(2,1)}, u32[]{:S(2)}) copy-start(bf16[1024,256]{1,0:T(8,128)(2,1)} %param.26) | copy-start | bytes 1572868
  7.2 26.4 %copy-start.13 = (bf16[1024]{0:T(1024)(128)(2,1)S(1)}, bf16[1024]{0:T(1024)(128)(2,1)}, u32[]{:S(2)}) copy-start(bf16[1024]{0:T(1024)(128)(2,1)} %param.25) | copy-start | bytes 6148
  7.2 26.4 %copy-start.15 = (bf16[256]{0:T(256)(128)(2,1)S(1)}, bf16[256]{0:T(256)(128)(2,1)}, u32[]{:S(2)}) copy-start(bf16[256]{0:T(256)(128)(2,1)} %param.27) | copy-start | bytes 1540
  7.2 26.4 %copy-start.11 = (bf16[128,13]{0,1:T(8,128)(2,1)S(1)}, bf16[128,13]{0,1:T(8,128)(2,1)}, u32[]{:S(2)}) copy-start(bf16[128,13]{0,1:T(8,128)(2,1)} %param.15) | copy-start | bytes 9988
  7.2 26.4 %copy-start.10 = (bf16[13,1024]{1,0:T(8,128)(2,1)S(1)}, bf16[13,1024]{1,0:T(8,128)(2,1)}, u32[]{:S(2)}) copy-start(bf16[13,1024]{1,0:T(8,128)(2,1)} %param.24) | copy-start | bytes 79876
  7.2 27.6 %copy-start.7 = (bf16[128,256]{1,0:T(8,128)(2,1)S(1)}, bf16[128,256]{1,0:T(8,128)(2,1)}, u32[]{:S(2)}) copy-start(bf16[128,256]{1,0:T(8,128)(2,1)} %param.29) | copy-start | bytes 196612
  7.2 1443.1 %all-gather.2.cloned.1.call-start = ((), (), s32[]{:S(2)}) async-start(), calls=%async_computation.4 | async-start | bytes 10506240 | tf_op jit(solution)/shard_map/all_gather | solution.py:56
  14.2 1436.1 %all-to-all-start = ((bf16[32,64,128]{2,1,0:T(8,128)(2,1)}), bf16[32,64,128]{2,1,0:T(8,128)(2,1)S(1)}, u32[]{:S(2)}, u32[]{:S(2)}) async-start(bf16[32,64,128]{2,1,0:T(8,128)(2,1)} %bitcast.69), calls=%async_computation | async-start | bytes 1048576 | tf_op jit(solution)/shard_map/all_to_all | solution.py:59
  33.6 1722.1 %reduce-scatter.3.cloned.1.call-start = ((), (), s32[]{:S(2)}) async-start(), calls=%async_computation.5 | async-start | bytes 11141120 | tf_op jit(solution)/shard_map/reduce_scatter | solution.py:118
  33.9 0.9 copy-start.5
  1450.3 1.6 slice-start.3
  1456.8 3.9 copy-start.8
  1456.8 4.0 copy-start.1
  1460.8 11.0 slice-start
  1460.9 11.0 slice-start.1
  1464.3 4.0 copy-start.4
  1464.3 4.2 copy-start.3
  1464.3 7.5 slice-start.2
  1486.5 4.8 copy-start.2
  1514.4 243.5 %copy-start.16 = (bf16[256]{0:T(256)(128)(2,1)S(1)}, bf16[256]{0:T(256)(128)(2,1)}, u32[]{:S(2)}) copy-start(bf16[256]{0:T(256)(128)(2,1)} %param.23) | copy-start | bytes 1540
  1514.4 244.3 %copy-start.9 = (bf16[256,256]{1,0:T(8,128)(2,1)S(1)}, bf16[256,256]{1,0:T(8,128)(2,1)}, u32[]{:S(2)}) copy-start(bf16[256,256]{1,0:T(8,128)(2,1)} %param.21) | copy-start | bytes 393220
  1514.4 244.3 %copy-start.17 = (f32[128,256]{1,0:T(8,128)S(1)}, f32[128,256]{1,0:T(8,128)}, u32[]{:S(2)}) copy-start(f32[128,256]{1,0:T(8,128)} %get-tuple-element.91) | copy-start | bytes 393220
  1514.5 244.5 %copy-start.14 = (f32[256]{0:T(256)S(1)}, f32[256]{0:T(256)}, u32[]{:S(2)}) copy-start(f32[256]{0:T(256)} %get-tuple-element.85) | copy-start | bytes 3076
  1514.5 244.6 %copy-start.6 = (f32[128,1024]{1,0:T(8,128)S(1)}, f32[128,1024]{1,0:T(8,128)}, u32[]{:S(2)}) copy-start(f32[128,1024]{1,0:T(8,128)} %copy-done.5) | copy-start | bytes 1572868
  1514.5 364.1 %copy-start.12 = (bf16[128,13]{0,1:T(8,128)(2,1)S(1)}, bf16[128,13]{0,1:T(8,128)(2,1)}, u32[]{:S(2)}) copy-start(bf16[128,13]{0,1:T(8,128)(2,1)} %param.15) | copy-start | bytes 9988
  1514.5 358.1 %reduce-scatter.5.cloned.1.call-start = ((), (), s32[]{:S(2)}) async-start(), calls=%async_computation.6 | async-start | bytes 1351680 | tf_op jit(solution)/shard_map/reduce_scatter | solution.py:121
  1874.2 119.4 %all-to-all-start.1 = ((bf16[16,16,640]{2,1,0:T(8,128)(2,1)}), bf16[16,16,640]{2,1,0:T(8,128)(2,1)S(1)}, u32[]{:S(2)}, u32[]{:S(2)}) async-start(bf16[16,16,640]{2,1,0:T(8,128)(2,1)} %stack.2), calls=%async_computation.3 | async-start | bytes 655360 | tf_op jit(solution)/shard_map/all_to_all | solution.py:126
Sparse Core Ops, SparseCore 0:
  11.9 1438.3 all-gather.1
  1514.6 241.0 reduce-scatter.2
  1760.1 112.4 reduce-scatter.4
